TPU v7x, 256 devices: a whole 4x4x8 slice. The times are simulated.
256 devices in a mesh: ta: 4 (over y), gz: 8 (over x, core), gy: 8 (over z).
Axes of the slice: x: 4, y: 4, z: 8, core: 2. Of those that a mesh axis runs over, the one named last changes fastest.
Arguments:
- source: float32 [2, 3, 8, 32, 1024], P(None, None, 'ta', 'gz', 'gy'), may hold values from -40 to 40
- fat_links: bfloat16 [2, 4, 2, 3, 3, 8, 32, 1024], P(None, None, None, None, None, 'ta', 'gz', 'gy'), may hold values from -1.25 to 1.25
- long_links: bfloat16 [2, 4, 2, 3, 3, 8, 32, 1024], P(None, None, None, None, None, 'ta', 'gz', 'gy'), may hold values from -0.625 to 0.625
Outputs:
- solution: float32 [2, 3, 8, 32, 1024], P(None, None, 'ta', 'gz', 'gy')
- true_residual: float32 [2, 3, 8, 32, 1024], P(None, None, 'ta', 'gz', 'gy')
All inputs are finite; a program needn't handle non-finite values.
Results may differ from a plain program's by a relative error of at most 0.00085.
Values may be sent and summed in bfloat16 or wider, within the bound.
A program may use at most 128 MiB of HBM per device.

v0:
```python
import functools

import jax
import jax.numpy as jnp
from jax import lax
from jax.experimental import pallas as pl
from jax.experimental.pallas import tpu as pltpu
from jax.sharding import PartitionSpec as P

NX = 32
BLOCKS = 4
MASS = 0.1
AXES = ("ta", "gz", "gy")
SIZES = {"ta": 4, "gz": 8, "gy": 8}
STAGES = ("gz", "ta", "gy")
DOTS = 9
TILE = (8, 128)


def iota(axis):
    return lax.broadcasted_iota(jnp.int32, TILE, axis)


class Grid:
    def __init__(self):
        sub, lane = iota(0), iota(1)
        self.row, self.z = sub // 4, sub % 4
        self.lane, self.x = lane, lane % NX
        self.odd = (self.z + lane // NX + self.x) % 2 == 1


def roll(field, shift, axis):
    return pltpu.roll(field, shift % TILE[axis], axis + 1)


def z_next(g, field):
    return jnp.where(g.z < 3, roll(field, -1, 0), roll(field, 3, 0))


def z_last(g, field):
    return jnp.where(g.z > 0, roll(field, 1, 0), roll(field, -3, 0))


def from_ahead(g, axis, hops, src, ahead, select):
    if axis == "ta":
        rolled = roll(jnp.where(g.row == 0, ahead, src), 4, 0)
        return jnp.where(select, rolled, src) if hops == 1 else jnp.where(select, ahead, rolled)
    if axis == "gz":
        if hops == 1:
            return z_next(g, jnp.where(g.z == 0, ahead, src))
        return z_last(g, jnp.where(g.z < 3, ahead, src))
    if axis == "gy":
        return roll(jnp.where(g.lane < hops * NX, ahead, src), -hops * NX, 1)
    return jnp.where(g.x < NX - hops, roll(src, -hops, 1), roll(src, NX - hops, 1))


def from_behind(g, axis, hops, src, behind, select):
    if axis == "ta":
        rolled = roll(jnp.where(g.row == 1, behind, src), 4, 0)
        return jnp.where(select, src, rolled) if hops == 1 else jnp.where(select, rolled, behind)
    if axis == "gz":
        if hops == 1:
            return z_last(g, jnp.where(g.z == 3, behind, src))
        return z_next(g, jnp.where(g.z > 0, behind, src))
    if axis == "gy":
        return roll(jnp.where(g.lane >= 128 - hops * NX, behind, src), hops * NX, 1)
    return jnp.where(g.x >= hops, roll(src, hops, 1), roll(src, hops - NX, 1))


def kernel(
    b_ref,
    fat_ref,
    long_ref,
    x_out,
    t_out,
    vec,
    prev,
    xs,
    odd_f,
    own,
    back,
    halo,
    rims,
    row,
    sums1,
    sums2,
    sums3,
    kept,
    halo_send,
    halo_recv,
    rim_send,
    rim_recv,
    sum_send,
    recv1,
    recv2,
    recv3,
):
    g = Grid()
    me = {a: lax.axis_index(a) for a in AXES}

    def at(axis, by):
        return {axis: lax.rem(me[axis] + (by % SIZES[axis]), SIZES[axis])}

    mesh_id = pl.DeviceIdType.MESH
    barrier = pltpu.get_barrier_semaphore()
    for axis in AXES:
        for by in range(1, SIZES[axis]):
            pl.semaphore_signal(barrier, inc=1, device_id=at(axis, by), device_id_type=mesh_id)
    pl.semaphore_wait(barrier, sum(SIZES[a] - 1 for a in AXES))

    def halo_copies(src, slot):
        copies = []
        for n, axis in enumerate(AXES):
            for side, by in enumerate((-1, 1)):
                copies.append(
                    pltpu.make_async_remote_copy(
                        src_ref=src,
                        dst_ref=halo.at[slot, n, side],
                        send_sem=halo_send.at[slot, n, side],
                        recv_sem=halo_recv.at[slot, n, side],
                        device_id=at(axis, by),
                        device_id_type=mesh_id,
                    )
                )
        return copies

    def rim_copies(p):
        copies = []
        for n, axis in enumerate(AXES):
            for kind, links in enumerate((fat_ref, long_ref)):
                copies.append(
                    pltpu.make_async_remote_copy(
                        src_ref=links.at[p, n],
                        dst_ref=rims.at[p, n, kind],
                        send_sem=rim_send.at[p, n, kind],
                        recv_sem=rim_recv.at[p, n, kind],
                        device_id=at(axis, 1),
                        device_id_type=mesh_id,
                    )
                )
        return copies

    def selected(dst):
        return g.odd if dst == 0 else jnp.logical_not(g.odd)

    rim = [rim_copies(0), rim_copies(1)]
    for copies in rim:
        for c in copies:
            c.start()
    for p in (1, 0):
        for mu in range(4):
            for kind, links in enumerate((fat_ref, long_ref)):
                own[p, 2 * mu + kind] = links[p, mu].astype(jnp.float32)
    for p in (0, 1):
        dst = 1 - p
        for mu in range(4):
            for kind in range(2):
                hops = 1 + 2 * kind
                axis = AXES[mu] if mu < 3 else "x"
                mine = own[p, 2 * mu + kind]
                if mu < 3:
                    rim[p][2 * mu + kind].wait_recv()
                    theirs = rims[p, mu, kind].astype(jnp.float32)
                else:
                    theirs = None
                back[dst, 2 * mu + kind] = from_behind(g, axis, hops, mine, theirs, selected(dst))
    for copies in rim:
        for c in copies:
            c.wait_send()

    def ahead_terms(acc, dst, k, v):
        re, im = acc
        vr, vi = v[:3], v[3:]
        for j in range(3):
            mr, mi = own[dst, k, pl.ds(j, 3, stride=3)], own[dst, k, pl.ds(9 + j, 3, stride=3)]
            re = re + mr * vr[j][None] - mi * vi[j][None]
            im = im + mr * vi[j][None] + mi * vr[j][None]
        return re, im

    def behind_terms(acc, dst, k, v):
        re, im = acc
        vr, vi = v[:3], v[3:]
        for i in range(3):
            mr, mi = back[dst, k, pl.ds(3 * i, 3)], back[dst, k, pl.ds(9 + 3 * i, 3)]
            re = re - mr * vr[i][None] - mi * vi[i][None]
            im = im - mr * vi[i][None] + mi * vr[i][None]
        return re, im

    def half(src_ref, dst):
        slot = dst
        copies = halo_copies(src_ref, slot)
        for c in copies:
            c.start()
        select = selected(dst)
        src = src_ref[...]
        zero = jnp.zeros((3, *TILE), jnp.float32)
        acc = (zero, zero)
        for axis, mu in (("x", 3), ("gz", 1), ("gy", 2), ("ta", 0)):
            ahead = behind = None
            if mu < 3:
                copies[2 * mu].wait_recv()
                copies[2 * mu + 1].wait_recv()
                ahead, behind = halo[slot, mu, 0], halo[slot, mu, 1]
            for kind in range(2):
                k, hops = 2 * mu + kind, 1 + 2 * kind
                acc = ahead_terms(acc, dst, k, from_ahead(g, axis, hops, src, ahead, select))
                acc = behind_terms(acc, dst, k, from_behind(g, axis, hops, src, behind, select))
        for c in copies:
            c.wait_send()
        return jnp.concatenate(acc, axis=0)

    def first_half(src):
        odd_f[...] = half(src, 1)

    def second_half(src):
        return MASS * src[...] - half(odd_f, 0)

    def stage_copies(blk, stage):
        axis = STAGES[stage]
        sums, recv = (sums1, sums2, sums3)[stage], (recv1, recv2, recv3)[stage]
        size = SIZES[axis]
        out, into = [], []
        for by in range(1, size):
            there = lax.rem(me[axis] + by, size)
            out.append(
                pltpu.make_async_remote_copy(
                    src_ref=row,
                    dst_ref=sums.at[blk, me[axis]],
                    send_sem=sum_send.at[by - 1],
                    recv_sem=recv.at[blk, me[axis]],
                    device_id={axis: there},
                    device_id_type=mesh_id,
                )
            )
            into.append(
                pltpu.make_async_remote_copy(
                    src_ref=row,
                    dst_ref=sums.at[blk, there],
                    send_sem=sum_send.at[by - 1],
                    recv_sem=recv.at[blk, there],
                    device_id={axis: there},
                    device_id_type=mesh_id,
                )
            )
        return out, into

    def stage_start(blk, stage, line):
        row[...] = line
        sums = (sums1, sums2, sums3)[stage]
        sums[blk, me[STAGES[stage]]] = line
        for c in stage_copies(blk, stage)[0]:
            c.start()

    def stage_end(blk, stage):
        out, into = stage_copies(blk, stage)
        for c in out:
            c.wait_send()
        for c in into:
            c.wait_recv()
        return jnp.sum((sums1, sums2, sums3)[stage][blk], axis=0)

    lane = lax.broadcasted_iota(jnp.int32, (1, 128), 1)

    def local_dots():
        r, w, q = vec[0], vec[1], vec[2]
        m, v = prev[0], prev[1]
        pairs = ((r, r), (r, w), (w, w), (w, q), (r, m), (w, m), (w, v), (m, m), (m, v))
        line = jnp.zeros((1, 128), jnp.float32)
        for n, (a, b) in enumerate(pairs):
            line = line + jnp.where(lane == n, jnp.sum(jnp.sum(a * b, axis=0)), 0.0)
        return line

    def coefficients(line):
        rr, rw, ww, wq, rm, wm, wv, mm, mv = (
            jnp.broadcast_to(jnp.sum(jnp.where(lane == n, line, 0.0)), TILE) for n in range(DOTS)
        )
        step = rr / rw
        u = 1.0 / (1.0 - step * rr * kept[...])
        f, h = -u * step, 1.0 - u
        rr1 = u * u * rr + f * f * ww + h * h * mm + 2.0 * (u * f * rw + u * h * rm + f * h * wm)
        rw1 = u * u * rw + f * f * wq + h * h * mv + 2.0 * (u * f * ww + u * h * wm + f * h * wv)
        step1 = rr1 / rw1
        u1 = 1.0 / (1.0 - step1 * rr1 / (step * rr * u))
        kept[...] = 1.0 / (step1 * rr1 * u1)
        return step, u, step1, u1

    def update(line, last):
        step, u, step1, u1 = coefficients(line)
        h, h1 = 1.0 - u, 1.0 - u1
        first = [
            u * (vec[k] - step * vec[k + 1]) + h * prev[k] for k in range(1 if last else 4)
        ]
        x, x0 = xs[0], xs[1]
        x1 = u * (x + step * vec[0]) + h * x0
        xs[1] = x1
        xs[0] = u1 * (x1 + step1 * first[0]) + h1 * x
        if not last:
            second = [u1 * (first[k] - step1 * first[k + 1]) + h1 * vec[k] for k in range(3)]
            for k in range(3):
                vec[k] = second[k]
            for k in range(4):
                prev[k] = first[k]

    vec[0] = b_ref[...]
    prev[...] = jnp.zeros_like(prev)
    xs[...] = jnp.zeros_like(xs)
    kept[...] = jnp.zeros_like(kept)

    def opening(k, carry):
        first_half(vec.at[k])
        vec[k + 1] = second_half(vec.at[k])
        return carry

    lax.fori_loop(0, 2, opening, 0)

    def block(blk, carry):
        stage_start(blk, 0, local_dots())
        first_half(vec.at[2])
        stage_start(blk, 1, stage_end(blk, 0))
        vec[3] = second_half(vec.at[2])
        stage_start(blk, 2, stage_end(blk, 1))
        first_half(vec.at[3])
        vec[4] = second_half(vec.at[3])
        update(stage_end(blk, 2), False)
        return carry

    lax.fori_loop(0, BLOCKS - 1, block, 0)
    line = local_dots()
    for stage in range(3):
        stage_start(BLOCKS - 1, stage, line)
        line = stage_end(BLOCKS - 1, stage)
    update(line, True)
    x_out[...] = xs[0]
    first_half(xs.at[0])
    t_out[...] = b_ref[...] - second_half(xs.at[0])


def per_device(source, fat_links, long_links):
    f32 = jnp.float32
    field = (6, *TILE)
    dma = pltpu.SemaphoreType.DMA
    fat = fat_links.reshape(2, 4, 18, *TILE)
    long = long_links.reshape(2, 4, 18, *TILE)
    vmem = pl.BlockSpec(memory_space=pltpu.VMEM)
    x, t = pl.pallas_call(
        kernel,
        out_shape=(jax.ShapeDtypeStruct(field, f32), jax.ShapeDtypeStruct(field, f32)),
        in_specs=[vmem] * 3,
        out_specs=(vmem, vmem),
        scratch_shapes=[
            pltpu.VMEM((5, *field), f32),
            pltpu.VMEM((4, *field), f32),
            pltpu.VMEM((2, *field), f32),
            pltpu.VMEM(field, f32),
            pltpu.VMEM((2, 8, 18, *TILE), f32),
            pltpu.VMEM((2, 8, 18, *TILE), f32),
            pltpu.VMEM((2, 3, 2, *field), f32),
            pltpu.VMEM((2, 3, 2, 18, *TILE), jnp.bfloat16),
            pltpu.VMEM((1, 128), f32),
            pltpu.VMEM((BLOCKS, SIZES[STAGES[0]], 1, 128), f32),
            pltpu.VMEM((BLOCKS, SIZES[STAGES[1]], 1, 128), f32),
            pltpu.VMEM((BLOCKS, SIZES[STAGES[2]], 1, 128), f32),
            pltpu.VMEM(TILE, f32),
            dma((2, 3, 2)),
            dma((2, 3, 2)),
            dma((2, 3, 2)),
            dma((2, 3, 2)),
            dma((7,)),
            dma((BLOCKS, SIZES[STAGES[0]])),
            dma((BLOCKS, SIZES[STAGES[1]])),
            dma((BLOCKS, SIZES[STAGES[2]])),
        ],
        compiler_params=pltpu.CompilerParams(
            collective_id=0, has_side_effects=True, vmem_limit_bytes=32 * 1024 * 1024
        ),
    )(source.reshape(field), fat, long)
    return x.reshape(source.shape), t.reshape(source.shape)


def solution(mesh):
    field = P(None, None, "ta", "gz", "gy")
    links = P(None, None, None, None, None, "ta", "gz", "gy")
    return jax.shard_map(
        per_device,
        mesh=mesh,
        in_specs=(field, links, links),
        out_specs=(field, field),
        check_vma=False,
    )
```

profile of v0, /device:TPU:1, one launch (start us, length us, event | category | flops | bytes accessed | tf_op | source)
XLA Modules:
  0.0 99.2 jit_solution(16141271911813016925)
XLA Ops:
  0.6 0.0 copy-start
  0.6 1.0 copy-done
  1.6 0.0 copy-start.1
  1.6 1.0 copy-done.1
  2.6 0.0 copy-start.2
  2.6 0.7 copy-done.2
  3.3 94.7 %shard_map.50 = (f32[6,8,128]{2,1,0:T(8,128)S(1)}, f32[6,8,128]{2,1,0:T(8,128)S(1)}) custom-call(f32[6,8,128]{2,1,0:T(8,128)S(1)} %bitcast.7, bf16[2,4,18,8,128]{4,3,2,1,0:T(8,128)(2,1)S(1)} %bitcast.5, bf16[2,4,18,8,128]{4,3,2,1,0:T(8,128)(2,1)S(1)} %bitcast.6), custom_call_target="tpu_custom_call" | custom-call | tf_op jit(solution)/shard_map/pallas_call | solution.py:345
  98.0 0.6 copy.7
  98.6 0.6 copy.8
Async XLA Ops:
  0.6 1.0 copy-start
  1.6 1.0 copy-start.1
  2.6 0.7 copy-start.2
where the time goes:
time: 99.4 us; the launch traced here: 99.2 us
  Pallas kernels  94.7 us (95%)
  local copies, waits for them, and re-layouts  3.87 us (4%)
    pallas_call x1, Pallas kernels, per_device(): pl.pallas_call(kernel, out_shape=(jax.ShapeDtypeStruct(field, f32), jax.S...  94.7 us
    unnamed x8, local copies, waits for them, and re-layouts  3.87 us

commit v1 on v0

v1 whole, which is shorter than its diff:
```python
import jax
import jax.numpy as jnp
from jax import lax
from jax.experimental import pallas as pl
from jax.experimental.pallas import tpu as pltpu
from jax.sharding import PartitionSpec as P

NX = 32
BLOCKS = 4
MASS = 0.1
AXES = ("ta", "gz", "gy")
SIZES = {"ta": 4, "gz": 8, "gy": 8}
MEMBERS = 16
DOTS = 9
TILE = (8, 128)


def iota(axis):
    return lax.broadcasted_iota(jnp.int32, TILE, axis)


class Grid:
    def __init__(self):
        sub, lane = iota(0), iota(1)
        self.row, self.z = sub // 4, sub % 4
        self.lane, self.x = lane, lane % NX
        self.odd = (self.z + lane // NX + self.x) % 2 == 1


def roll(field, shift, axis):
    return pltpu.roll(field, shift % TILE[axis], axis + 1)


def z_next(g, field):
    return jnp.where(g.z < 3, roll(field, -1, 0), roll(field, 3, 0))


def z_last(g, field):
    return jnp.where(g.z > 0, roll(field, 1, 0), roll(field, -3, 0))


def from_ahead(g, axis, hops, src, ahead, select):
    if axis == "ta":
        rolled = roll(jnp.where(g.row == 0, ahead, src), 4, 0)
        return jnp.where(select, rolled, src) if hops == 1 else jnp.where(select, ahead, rolled)
    if axis == "gz":
        if hops == 1:
            return z_next(g, jnp.where(g.z == 0, ahead, src))
        return z_last(g, jnp.where(g.z < 3, ahead, src))
    if axis == "gy":
        return roll(jnp.where(g.lane < hops * NX, ahead, src), -hops * NX, 1)
    return jnp.where(g.x < NX - hops, roll(src, -hops, 1), roll(src, NX - hops, 1))


def from_behind(g, axis, hops, src, behind, select):
    if axis == "ta":
        rolled = roll(jnp.where(g.row == 1, behind, src), 4, 0)
        return jnp.where(select, src, rolled) if hops == 1 else jnp.where(select, rolled, behind)
    if axis == "gz":
        if hops == 1:
            return z_last(g, jnp.where(g.z == 3, behind, src))
        return z_next(g, jnp.where(g.z > 0, behind, src))
    if axis == "gy":
        return roll(jnp.where(g.lane >= 128 - hops * NX, behind, src), hops * NX, 1)
    return jnp.where(g.x >= hops, roll(src, hops, 1), roll(src, hops - NX, 1))


def kernel(
    b_hbm,
    fat_hbm,
    long_hbm,
    x_out,
    t_out,
    fat_ref,
    long_ref,
    src_b,
    vec,
    prev,
    xs,
    images,
    odd_f,
    own,
    back,
    halo,
    rims,
    row,
    sums,
    kept,
    shift,
    load,
    halo_send,
    halo_recv,
    rim_send,
    rim_recv,
    sum_send,
    sum_recv,
):
    g = Grid()
    me = {a: lax.axis_index(a) for a in AXES}
    mesh_id = pl.DeviceIdType.MESH

    def at(axis, by):
        return {axis: lax.rem(me[axis] + (by % SIZES[axis]), SIZES[axis])}

    low, high = lax.rem(me["ta"], 2), me["ta"] // 2
    groups = (("gz", low, me["ta"] + 1 - 2 * low), ("gy", high, 3 - me["ta"]))

    def peers(stage):
        axis, bit, partner = groups[stage]
        for by in range(SIZES[axis]):
            there = lax.rem(me[axis] + by, SIZES[axis])
            if by:
                yield {axis: there}, 2 * there + bit
            yield {axis: there, "ta": partner}, 2 * there + 1 - bit

    def my_place(stage):
        axis, bit, _ = groups[stage]
        return 2 * me[axis] + bit

    barrier = pltpu.get_barrier_semaphore()
    for axis in AXES:
        for by in (-1, 1):
            pl.semaphore_signal(barrier, inc=1, device_id=at(axis, by), device_id_type=mesh_id)
    loads = [
        pltpu.make_async_copy(a, c, load.at[n])
        for n, (a, c) in enumerate(((b_hbm, src_b), (fat_hbm, fat_ref), (long_hbm, long_ref)))
    ]
    for c in loads:
        c.start()
    pl.semaphore_wait(barrier, 2 * len(AXES))

    def halo_copies(fields, slot):
        copies = []
        for n, axis in enumerate(AXES):
            for side, by in enumerate((-1, 1)):
                for f, src in enumerate(fields):
                    copies.append(
                        pltpu.make_async_remote_copy(
                            src_ref=src,
                            dst_ref=halo.at[slot, f, n, side],
                            send_sem=halo_send.at[slot, f, n, side],
                            recv_sem=halo_recv.at[slot, f, n, side],
                            device_id=at(axis, by),
                            device_id_type=mesh_id,
                        )
                    )
        return copies

    def rim_copies(p):
        copies = []
        for n, axis in enumerate(AXES):
            for kind, links in enumerate((fat_ref, long_ref)):
                copies.append(
                    pltpu.make_async_remote_copy(
                        src_ref=links.at[p, n],
                        dst_ref=rims.at[p, n, kind],
                        send_sem=rim_send.at[p, n, kind],
                        recv_sem=rim_recv.at[p, n, kind],
                        device_id=at(axis, 1),
                        device_id_type=mesh_id,
                    )
                )
        return copies

    def selected(dst):
        return g.odd if dst == 0 else jnp.logical_not(g.odd)

    rim = [rim_copies(0), rim_copies(1)]

    def own_links(p):
        for mu in range(4):
            for kind, links in enumerate((fat_ref, long_ref)):
                own[p, 2 * mu + kind] = links[p, mu].astype(jnp.float32)

    def back_links(p):
        dst = 1 - p
        for mu in (3, 1, 2, 0):
            for kind in range(2):
                theirs = None
                if mu < 3:
                    rim[p][2 * mu + kind].wait_recv()
                    theirs = rims[p, mu, kind].astype(jnp.float32)
                axis = AXES[mu] if mu < 3 else "x"
                back[dst, 2 * mu + kind] = from_behind(
                    g, axis, 1 + 2 * kind, own[p, 2 * mu + kind], theirs, selected(dst)
                )

    def ahead_terms(acc, dst, k, v):
        re, im = acc
        vr, vi = v[:3], v[3:]
        for j in range(3):
            mr, mi = own[dst, k, pl.ds(j, 3, stride=3)], own[dst, k, pl.ds(9 + j, 3, stride=3)]
            re = re + mr * vr[j][None] - mi * vi[j][None]
            im = im + mr * vi[j][None] + mi * vr[j][None]
        return re, im

    def behind_terms(acc, dst, k, v):
        re, im = acc
        vr, vi = v[:3], v[3:]
        for i in range(3):
            mr, mi = back[dst, k, pl.ds(3 * i, 3)], back[dst, k, pl.ds(9 + 3 * i, 3)]
            re = re - mr * vr[i][None] - mi * vi[i][None]
            im = im - mr * vi[i][None] + mi * vr[i][None]
        return re, im

    def half(fields, dst, between=None):
        slot = dst
        copies = halo_copies(fields, slot)
        for c in copies:
            c.start()
        if between is not None:
            between()
        select = selected(dst)
        zero = jnp.zeros((3, *TILE), jnp.float32)
        accs = [(zero, zero) for _ in fields]
        per_axis = 2 * len(fields)
        for axis, mu in (("x", 3), ("gz", 1), ("gy", 2), ("ta", 0)):
            if mu < 3:
                for c in copies[per_axis * mu : per_axis * (mu + 1)]:
                    c.wait_recv()
            for f, field in enumerate(fields):
                src, acc = field[...], accs[f]
                ahead = behind = None
                if mu < 3:
                    ahead, behind = halo[slot, f, mu, 0], halo[slot, f, mu, 1]
                for kind in range(2):
                    k, hops = 2 * mu + kind, 1 + 2 * kind
                    acc = ahead_terms(acc, dst, k, from_ahead(g, axis, hops, src, ahead, select))
                    acc = behind_terms(acc, dst, k, from_behind(g, axis, hops, src, behind, select))
                accs[f] = acc
        for c in copies:
            c.wait_send()
        return [jnp.concatenate(acc, axis=0) for acc in accs]

    def first_half(fields, between=None):
        for f, value in enumerate(half(fields, 1, between)):
            odd_f[f] = value

    def second_half(fields, diagonal, between=None):
        odds = [odd_f.at[f] for f in range(len(fields))]
        return [diagonal * v[...] - d for v, d in zip(fields, half(odds, 0, between))]

    def stage_copies(blk, stage, place_of):
        copies = []
        for n, (device, place) in enumerate(peers(stage)):
            spot = my_place(stage) if place_of == "mine" else place
            copies.append(
                pltpu.make_async_remote_copy(
                    src_ref=row,
                    dst_ref=sums.at[stage, blk, spot],
                    send_sem=sum_send.at[n],
                    recv_sem=sum_recv.at[stage, blk, spot],
                    device_id=device,
                    device_id_type=mesh_id,
                )
            )
        return copies

    def stage_start(blk, stage, line):
        row[...] = line
        sums[stage, blk, my_place(stage)] = line
        for c in stage_copies(blk, stage, "mine"):
            c.start()

    def stage_end(blk, stage):
        for c in stage_copies(blk, stage, "theirs"):
            c.wait_send()
            c.wait_recv()
        return jnp.sum(sums[stage, blk], axis=0)

    lane = lax.broadcasted_iota(jnp.int32, (1, 128), 1)

    def local_dots():
        r, w, q = vec[0], vec[1], vec[2]
        m, v = prev[0], prev[1]
        pairs = ((r, r), (r, w), (w, w), (w, q), (r, m), (w, m), (w, v), (m, m), (m, v))
        line = jnp.zeros((1, 128), jnp.float32)
        for n, (a, b) in enumerate(pairs):
            line = line + jnp.where(lane == n, jnp.sum(jnp.sum(a * b, axis=0)), 0.0)
        return line

    def coefficients(line):
        rr, rw, ww, wq, rm, wm, wv, mm, mv = (
            jnp.broadcast_to(jnp.sum(jnp.where(lane == n, line, 0.0)), TILE) for n in range(DOTS)
        )
        c = shift[...]
        step = rr / (rw + c * rr)
        scale = 1.0 / (1.0 - step * rr * kept[...])
        u, f, h = scale * (1.0 - step * c), -scale * step, 1.0 - scale
        rr1 = u * u * rr + f * f * ww + h * h * mm + 2.0 * (u * f * rw + u * h * rm + f * h * wm)
        rw1 = u * u * rw + f * f * wq + h * h * mv + 2.0 * (u * f * ww + u * h * wm + f * h * wv)
        mean1 = (rw1 + c * rr1) / rr1
        step1 = 1.0 / mean1
        scale1 = 1.0 / (1.0 - step1 * rr1 / (step * rr * scale))
        u1, f1, h1 = scale1 * (1.0 - step1 * c), -scale1 * step1, 1.0 - scale1
        kept[...] = 1.0 / (step1 * rr1 * scale1)
        return (step, scale, u, f, h), (step1, scale1, u1, f1, h1), mean1

    def update(line):
        (step, scale, u, f, h), (step1, scale1, u1, f1, h1), mean1 = coefficients(line)
        first = [u * vec[k] + f * vec[k + 1] + h * prev[k] for k in range(4)]
        second = [u1 * first[k] + f1 * first[k + 1] + h1 * vec[k] for k in range(3)]
        x, x0 = xs[0], xs[1]
        x1 = scale * (x + step * vec[0]) + h * x0
        xs[1] = x1
        xs[0] = scale1 * (x1 + step1 * first[0]) + h1 * x
        d = mean1 - shift[...]
        shift[...] = mean1
        for stack, place in ((second, vec), (first, prev)):
            for k in range(len(stack)):
                place[k] = stack[0]
                stack = [b - d * a for a, b in zip(stack, stack[1:])]

    def last_update(line):
        (step, scale, u, f, h), (step1, scale1, u1, f1, h1), _ = coefficients(line)
        c = shift[...]
        r, w, q, m, v = vec[0], vec[1], vec[2], prev[0], prev[1]
        x, x0, ax, ax0 = xs[0], xs[1], images[0], images[1]
        r1 = u * r + f * w + h * m
        x1 = scale * (x + step * r) + h * x0
        x_out[...] = scale1 * (x1 + step1 * r1) + h1 * x
        ar = w + c * r
        ar1 = u * ar + f * (q + c * w) + h * (v + c * m)
        ax1 = scale * (ax + step * ar) + h * ax0
        t_out[...] = src_b[...] - (scale1 * (ax1 + step1 * ar1) + h1 * ax)

    loads[0].wait()
    vec[0] = src_b[...]
    prev[...] = jnp.zeros_like(prev)
    xs[...] = jnp.zeros_like(xs)
    kept[...] = jnp.zeros_like(kept)
    shift[...] = jnp.zeros_like(shift)

    def links_for_first():
        loads[1].wait()
        loads[2].wait()
        for copies in rim:
            for c in copies:
                c.start()
        own_links(0)
        own_links(1)
        back_links(0)

    def links_for_second():
        back_links(1)
        for copies in rim:
            for c in copies:
                c.wait_send()

    first_half([src_b], links_for_first)
    (vec[1],) = second_half([src_b], MASS, links_for_second)
    first_half([vec.at[1]])
    (vec[2],) = second_half([vec.at[1]], MASS)

    def block(blk, carry):
        diagonal = MASS - shift[...]
        stage_start(blk, 0, local_dots())
        first_half([vec.at[2]])
        (vec[3],) = second_half([vec.at[2]], diagonal)
        stage_start(blk, 1, stage_end(blk, 0))
        first_half([vec.at[3]])
        (vec[4],) = second_half([vec.at[3]], diagonal)
        update(stage_end(blk, 1))
        return carry

    lax.fori_loop(0, BLOCKS - 1, block, 0)
    stage_start(BLOCKS - 1, 0, local_dots())
    both = [xs.at[0], xs.at[1]]
    first_half(both)
    stage_start(BLOCKS - 1, 1, stage_end(BLOCKS - 1, 0))
    images[0], images[1] = second_half(both, MASS)
    last_update(stage_end(BLOCKS - 1, 1))


def per_device(source, fat_links, long_links):
    f32 = jnp.float32
    field = (6, *TILE)
    dma = pltpu.SemaphoreType.DMA
    fat = fat_links.reshape(2, 4, 18, *TILE)
    long = long_links.reshape(2, 4, 18, *TILE)
    vmem = pl.BlockSpec(memory_space=pltpu.VMEM)
    hbm = pl.BlockSpec(memory_space=pltpu.HBM)
    x, t = pl.pallas_call(
        kernel,
        out_shape=(jax.ShapeDtypeStruct(field, f32), jax.ShapeDtypeStruct(field, f32)),
        in_specs=[hbm] * 3,
        out_specs=(vmem, vmem),
        scratch_shapes=[
            pltpu.VMEM(fat.shape, fat.dtype),
            pltpu.VMEM(long.shape, long.dtype),
            pltpu.VMEM(field, f32),
            pltpu.VMEM((5, *field), f32),
            pltpu.VMEM((4, *field), f32),
            pltpu.VMEM((2, *field), f32),
            pltpu.VMEM((2, *field), f32),
            pltpu.VMEM((2, *field), f32),
            pltpu.VMEM((2, 8, 18, *TILE), f32),
            pltpu.VMEM((2, 8, 18, *TILE), f32),
            pltpu.VMEM((2, 2, 3, 2, *field), f32),
            pltpu.VMEM((2, 3, 2, 18, *TILE), jnp.bfloat16),
            pltpu.VMEM((1, 128), f32),
            pltpu.VMEM((2, BLOCKS, MEMBERS, 1, 128), f32),
            pltpu.VMEM(TILE, f32),
            pltpu.VMEM(TILE, f32),
            dma((3,)),
            dma((2, 2, 3, 2)),
            dma((2, 2, 3, 2)),
            dma((2, 3, 2)),
            dma((2, 3, 2)),
            dma((MEMBERS - 1,)),
            dma((2, BLOCKS, MEMBERS)),
        ],
        compiler_params=pltpu.CompilerParams(
            collective_id=0, has_side_effects=True
        ),
    )(source.reshape(field), fat, long)
    return x.reshape(source.shape), t.reshape(source.shape)


def solution(mesh):
    field = P(None, None, "ta", "gz", "gy")
    links = P(None, None, None, None, None, "ta", "gz", "gy")
    return jax.shard_map(
        per_device,
        mesh=mesh,
        in_specs=(field, links, links),
        out_specs=(field, field),
        check_vma=False,
    )
```

time: 99.4 us -> 85 us (0.86)
  Pallas kernels: 94.7 us -> 82.3 us
  local copies, waits for them, and re-layouts: 3.87 us -> 1.96 us
    pallas_call x1, Pallas kernels: 94.7 us -> 82.3 us  [per_device(): pl.pallas_call(kernel, out_shape=(jax.ShapeDtypeStruct(field, f32), jax.S...]
    unnamed x8 -> x4, local copies, waits for them, and re-layouts: 3.87 us -> 1.96 us
where the time goes in v1:
time: 85 us; the launch traced here: 84.9 us
  Pallas kernels  82.3 us (97%)
  local copies, waits for them, and re-layouts  1.96 us (2%)
    pallas_call x1, Pallas kernels, per_device(): pl.pallas_call(kernel, out_shape=(jax.ShapeDtypeStruct(field, f32), jax.S...  82.3 us
    unnamed x4, local copies, waits for them, and re-layouts  1.96 us

profile of v1, /device:TPU:1, one launch (start us, length us, event | category | flops | bytes accessed | tf_op | source)
XLA Modules:
  0.0 84.9 jit_solution(10819403418013471508)
XLA Ops:
  0.6 82.3 %shard_map.50 = (f32[6,8,128]{2,1,0:T(8,128)}, f32[6,8,128]{2,1,0:T(8,128)}) custom-call(f32[6,8,128]{2,1,0:T(8,128)} %bitcast.7, bf16[2,4,18,8,128]{4,3,2,1,0:T(8,128)(2,1)} %bitcast.5, bf16[2,4,18,8,128]{4,3,2,1,0:T(8,128)(2,1)} %bitcast.6), custom_call_target="tpu_custom_call" | custom-call | tf_op jit(solution)/shard_map/pallas_call | solution.py:383
  82.9 0.0 copy-start
  82.9 1.4 %copy.7 = f32[2,3,2,4,128]{4,3,2,1,0:T(4,128)} copy(f32[2,3,2,4,128]{4,3,2,1,0:T(4,128)} %bitcast.9) | data formatting | bytes 49152
  84.3 0.0 copy-done
  84.3 0.6 copy.8
Async XLA Ops:
  82.9 1.4 %copy-start = (f32[6,8,128]{2,1,0:T(8,128)S(1)}, f32[6,8,128]{2,1,0:T(8,128)}, u32[]{:S(2)}) copy-start(f32[6,8,128]{2,1,0:T(8,128)} %get-tuple-element.5) | copy-start | bytes 73732

commit v2 on v1

--- a/solution.py
+++ b/solution.py
@@ -31,38 +31,42 @@
     return pltpu.roll(field, shift % TILE[axis], axis + 1)
 
 
-def z_next(g, field):
-    return jnp.where(g.z < 3, roll(field, -1, 0), roll(field, 3, 0))
-
-
-def z_last(g, field):
-    return jnp.where(g.z > 0, roll(field, 1, 0), roll(field, -3, 0))
-
-
-def from_ahead(g, axis, hops, src, ahead, select):
+def turn(g, axis, kind, field, select):
     if axis == "ta":
-        rolled = roll(jnp.where(g.row == 0, ahead, src), 4, 0)
-        return jnp.where(select, rolled, src) if hops == 1 else jnp.where(select, ahead, rolled)
+        rolled = roll(field, 4, 0)
+        return jnp.where(select, rolled, field) if kind == 0 else jnp.where(select, field, rolled)
     if axis == "gz":
-        if hops == 1:
-            return z_next(g, jnp.where(g.z == 0, ahead, src))
-        return z_last(g, jnp.where(g.z < 3, ahead, src))
-    if axis == "gy":
-        return roll(jnp.where(g.lane < hops * NX, ahead, src), -hops * NX, 1)
-    return jnp.where(g.x < NX - hops, roll(src, -hops, 1), roll(src, NX - hops, 1))
-
-
-def from_behind(g, axis, hops, src, behind, select):
+        if kind == 0:
+            return jnp.where(g.z < 3, roll(field, -1, 0), roll(field, 3, 0))
+        return jnp.where(g.z > 0, roll(field, 1, 0), roll(field, -3, 0))
+    return roll(field, -NX if kind == 0 else NX, 1)
+
+
+def across(g, axis, kind, ahead, behind, select):
     if axis == "ta":
-        rolled = roll(jnp.where(g.row == 1, behind, src), 4, 0)
-        return jnp.where(select, src, rolled) if hops == 1 else jnp.where(select, rolled, behind)
+        rolled = roll(jnp.where(g.row == 0, ahead, behind), 4, 0)
+        return jnp.where(select, rolled, behind) if kind == 0 else jnp.where(select, ahead, rolled)
     if axis == "gz":
-        if hops == 1:
-            return z_last(g, jnp.where(g.z == 3, behind, src))
-        return z_next(g, jnp.where(g.z > 0, behind, src))
-    if axis == "gy":
-        return roll(jnp.where(g.lane >= 128 - hops * NX, behind, src), hops * NX, 1)
-    return jnp.where(g.x >= hops, roll(src, hops, 1), roll(src, hops - NX, 1))
+        mixed = jnp.where(g.z == 0 if kind == 0 else g.z < 3, ahead, behind)
+    else:
+        mixed = jnp.where(g.lane < (NX if kind == 0 else 3 * NX), ahead, behind)
+    return turn(g, axis, kind, mixed, select)
+
+
+def inside(g, axis, kind, select):
+    if axis == "ta":
+        unselected = jnp.logical_not(select)
+        first = g.row == 0
+        return jnp.logical_or(unselected, first) if kind == 0 else jnp.logical_and(unselected, first)
+    if axis == "gz":
+        return g.z < 3 if kind == 0 else g.z == 0
+    return g.lane < (3 * NX if kind == 0 else NX)
+
+
+def along_x(g, by, field):
+    if by > 0:
+        return jnp.where(g.x < NX - by, roll(field, -by, 1), roll(field, NX - by, 1))
+    return jnp.where(g.x >= -by, roll(field, -by, 1), roll(field, -by - NX, 1))
 
 
 def kernel(
@@ -79,8 +83,7 @@
     xs,
     images,
     odd_f,
-    own,
-    back,
+    mats,
     halo,
     rims,
     row,
@@ -167,78 +170,96 @@
 
     rim = [rim_copies(0), rim_copies(1)]
 
-    def own_links(p):
-        for mu in range(4):
-            for kind, links in enumerate((fat_ref, long_ref)):
-                own[p, 2 * mu + kind] = links[p, mu].astype(jnp.float32)
-
-    def back_links(p):
-        dst = 1 - p
-        for mu in (3, 1, 2, 0):
+    def plain(links, p, mu):
+        columns = [links[p, mu, pl.ds(9 * part + j, 3, stride=3)] for part in (0, 1) for j in range(3)]
+        return jnp.concatenate(columns, axis=0).astype(jnp.float32)
+
+    def minus_adjoint(links):
+        links = links.astype(jnp.float32)
+        return jnp.concatenate([-links[:9], links[9:]], axis=0)
+
+    kinds = (fat_ref, long_ref)
+    X_HOPS = ((0, 1), (1, 3), (0, -1), (1, -3))
+
+    def local_matrices(dst):
+        select = selected(dst)
+        for n, (kind, by) in enumerate(X_HOPS):
+            if by > 0:
+                mats[dst, n] = plain(kinds[kind], dst, 3)
+            else:
+                links = kinds[kind][1 - dst, 3].astype(jnp.float32)
+                mats[dst, n] = minus_adjoint(along_x(g, by, links))
+        for mu, axis in enumerate(AXES):
             for kind in range(2):
-                theirs = None
-                if mu < 3:
-                    rim[p][2 * mu + kind].wait_recv()
-                    theirs = rims[p, mu, kind].astype(jnp.float32)
-                axis = AXES[mu] if mu < 3 else "x"
-                back[dst, 2 * mu + kind] = from_behind(
-                    g, axis, 1 + 2 * kind, own[p, 2 * mu + kind], theirs, selected(dst)
+                links = kinds[1 - kind][1 - dst, mu].astype(jnp.float32)
+                mats[dst, 4 + 4 * mu + kind] = jnp.where(
+                    inside(g, axis, kind, select),
+                    plain(kinds[kind], dst, mu),
+                    minus_adjoint(turn(g, axis, kind, links, select)),
                 )
 
-    def ahead_terms(acc, dst, k, v):
+    def border_matrices(dst):
+        select = selected(dst)
+        for mu, axis in enumerate(AXES):
+            for kind in range(2):
+                rim[1 - dst][2 * mu + 1 - kind].wait_recv()
+                links = rims[1 - dst, mu, 1 - kind].astype(jnp.float32)
+                mats[dst, 6 + 4 * mu + kind] = jnp.where(
+                    inside(g, axis, kind, select),
+                    minus_adjoint(turn(g, axis, kind, links, select)),
+                    plain(kinds[kind], dst, mu),
+                )
+
+    def times(acc, dst, k, v):
         re, im = acc
         vr, vi = v[:3], v[3:]
         for j in range(3):
-            mr, mi = own[dst, k, pl.ds(j, 3, stride=3)], own[dst, k, pl.ds(9 + j, 3, stride=3)]
+            mr, mi = mats[dst, k, pl.ds(3 * j, 3)], mats[dst, k, pl.ds(9 + 3 * j, 3)]
             re = re + mr * vr[j][None] - mi * vi[j][None]
             im = im + mr * vi[j][None] + mi * vr[j][None]
         return re, im
 
-    def behind_terms(acc, dst, k, v):
-        re, im = acc
-        vr, vi = v[:3], v[3:]
-        for i in range(3):
-            mr, mi = back[dst, k, pl.ds(3 * i, 3)], back[dst, k, pl.ds(9 + 3 * i, 3)]
-            re = re - mr * vr[i][None] - mi * vi[i][None]
-            im = im - mr * vi[i][None] + mi * vr[i][None]
-        return re, im
-
-    def half(fields, dst, between=None):
+    def half(fields, dst, hook=None, border_hook=None):
         slot = dst
         copies = halo_copies(fields, slot)
         for c in copies:
             c.start()
-        if between is not None:
-            between()
+        if hook is not None:
+            hook()
         select = selected(dst)
-        zero = jnp.zeros((3, *TILE), jnp.float32)
-        accs = [(zero, zero) for _ in fields]
+        accs = []
+        for field in fields:
+            src = field[...]
+            acc = (jnp.zeros((3, *TILE), jnp.float32),) * 2
+            for n, (_, by) in enumerate(X_HOPS):
+                acc = times(acc, dst, n, along_x(g, by, src))
+            for mu, axis in enumerate(AXES):
+                for kind in range(2):
+                    acc = times(acc, dst, 4 + 4 * mu + kind, turn(g, axis, kind, src, select))
+            accs.append(acc)
+        if border_hook is not None:
+            border_hook()
         per_axis = 2 * len(fields)
-        for axis, mu in (("x", 3), ("gz", 1), ("gy", 2), ("ta", 0)):
-            if mu < 3:
-                for c in copies[per_axis * mu : per_axis * (mu + 1)]:
-                    c.wait_recv()
-            for f, field in enumerate(fields):
-                src, acc = field[...], accs[f]
-                ahead = behind = None
-                if mu < 3:
-                    ahead, behind = halo[slot, f, mu, 0], halo[slot, f, mu, 1]
+        for axis, mu in (("gz", 1), ("gy", 2), ("ta", 0)):
+            for c in copies[per_axis * mu : per_axis * (mu + 1)]:
+                c.wait_recv()
+            for f in range(len(fields)):
+                ahead, behind = halo[slot, f, mu, 0], halo[slot, f, mu, 1]
                 for kind in range(2):
-                    k, hops = 2 * mu + kind, 1 + 2 * kind
-                    acc = ahead_terms(acc, dst, k, from_ahead(g, axis, hops, src, ahead, select))
-                    acc = behind_terms(acc, dst, k, from_behind(g, axis, hops, src, behind, select))
-                accs[f] = acc
+                    v = across(g, axis, kind, ahead, behind, select)
+                    accs[f] = times(accs[f], dst, 6 + 4 * mu + kind, v)
         for c in copies:
             c.wait_send()
         return [jnp.concatenate(acc, axis=0) for acc in accs]
 
-    def first_half(fields, between=None):
-        for f, value in enumerate(half(fields, 1, between)):
+    def first_half(fields, hook=None, border_hook=None):
+        for f, value in enumerate(half(fields, 1, hook, border_hook)):
             odd_f[f] = value
 
-    def second_half(fields, diagonal, between=None):
+    def second_half(fields, diagonal, hook=None, border_hook=None):
         odds = [odd_f.at[f] for f in range(len(fields))]
-        return [diagonal * v[...] - d for v, d in zip(fields, half(odds, 0, between))]
+        values = half(odds, 0, hook, border_hook)
+        return [diagonal * v[...] - d for v, d in zip(fields, values)]
 
     def stage_copies(blk, stage, place_of):
         copies = []
@@ -296,16 +317,24 @@
         kept[...] = 1.0 / (step1 * rr1 * scale1)
         return (step, scale, u, f, h), (step1, scale1, u1, f1, h1), mean1
 
-    def update(line):
+    def early_update(line):
         (step, scale, u, f, h), (step1, scale1, u1, f1, h1), mean1 = coefficients(line)
-        first = [u * vec[k] + f * vec[k + 1] + h * prev[k] for k in range(4)]
-        second = [u1 * first[k] + f1 * first[k + 1] + h1 * vec[k] for k in range(3)]
+        first = [u * vec[k] + f * vec[k + 1] + h * prev[k] for k in range(3)]
+        second = [u1 * first[k] + f1 * first[k + 1] + h1 * vec[k] for k in range(2)]
         x, x0 = xs[0], xs[1]
         x1 = scale * (x + step * vec[0]) + h * x0
         xs[1] = x1
         xs[0] = scale1 * (x1 + step1 * first[0]) + h1 * x
         d = mean1 - shift[...]
         shift[...] = mean1
+        half_first3 = u * vec[3] + h * prev[3]
+        half_second2 = u1 * first[2] + h1 * vec[2]
+        return d, f, f1, first, second, half_first3, half_second2
+
+    def late_update(parts, fourth):
+        d, f, f1, first, second, half_first3, half_second2 = parts
+        first = first + [half_first3 + f * fourth]
+        second = second + [half_second2 + f1 * first[3]]
         for stack, place in ((second, vec), (first, prev)):
             for k in range(len(stack)):
                 place[k] = stack[0]
@@ -331,45 +360,47 @@
     kept[...] = jnp.zeros_like(kept)
     shift[...] = jnp.zeros_like(shift)
 
-    def links_for_first():
+    def first_links():
         loads[1].wait()
         loads[2].wait()
         for copies in rim:
             for c in copies:
                 c.start()
-        own_links(0)
-        own_links(1)
-        back_links(0)
-
-    def links_for_second():
-        back_links(1)
+        local_matrices(1)
+
+    def second_borders():
+        border_matrices(0)
         for copies in rim:
             for c in copies:
                 c.wait_send()
 
-    first_half([src_b], links_for_first)
-    (vec[1],) = second_half([src_b], MASS, links_for_second)
+    first_half([src_b], first_links, lambda: border_matrices(1))
+    (vec[1],) = second_half([src_b], MASS, lambda: local_matrices(0), second_borders)
     first_half([vec.at[1]])
     (vec[2],) = second_half([vec.at[1]], MASS)
 
     def block(blk, carry):
         diagonal = MASS - shift[...]
-        stage_start(blk, 0, local_dots())
-        first_half([vec.at[2]])
-        (vec[3],) = second_half([vec.at[2]], diagonal)
-        stage_start(blk, 1, stage_end(blk, 0))
+        first_half([vec.at[2]], lambda: stage_start(blk, 0, local_dots()))
+        (vec[3],) = second_half(
+            [vec.at[2]], diagonal, lambda: stage_start(blk, 1, stage_end(blk, 0))
+        )
         first_half([vec.at[3]])
-        (vec[4],) = second_half([vec.at[3]], diagonal)
-        update(stage_end(blk, 1))
+        parts = []
+        (fourth,) = second_half(
+            [vec.at[3]], diagonal, lambda: parts.extend(early_update(stage_end(blk, 1)))
+        )
+        late_update(parts, fourth)
         return carry
 
     lax.fori_loop(0, BLOCKS - 1, block, 0)
-    stage_start(BLOCKS - 1, 0, local_dots())
+    last = BLOCKS - 1
     both = [xs.at[0], xs.at[1]]
-    first_half(both)
-    stage_start(BLOCKS - 1, 1, stage_end(BLOCKS - 1, 0))
-    images[0], images[1] = second_half(both, MASS)
-    last_update(stage_end(BLOCKS - 1, 1))
+    first_half(both, lambda: stage_start(last, 0, local_dots()))
+    images[0], images[1] = second_half(
+        both, MASS, lambda: stage_start(last, 1, stage_end(last, 0))
+    )
+    last_update(stage_end(last, 1))
 
 
 def per_device(source, fat_links, long_links):
@@ -389,13 +420,12 @@
             pltpu.VMEM(fat.shape, fat.dtype),
             pltpu.VMEM(long.shape, long.dtype),
             pltpu.VMEM(field, f32),
-            pltpu.VMEM((5, *field), f32),
+            pltpu.VMEM((4, *field), f32),
             pltpu.VMEM((4, *field), f32),
             pltpu.VMEM((2, *field), f32),
             pltpu.VMEM((2, *field), f32),
             pltpu.VMEM((2, *field), f32),
-            pltpu.VMEM((2, 8, 18, *TILE), f32),
-            pltpu.VMEM((2, 8, 18, *TILE), f32),
+            pltpu.VMEM((2, 16, 18, *TILE), f32),
             pltpu.VMEM((2, 2, 3, 2, *field), f32),
             pltpu.VMEM((2, 3, 2, 18, *TILE), jnp.bfloat16),
             pltpu.VMEM((1, 128), f32),

time: 85 us -> 82.3 us (0.968)
  Pallas kernels: 82.3 us -> 79.6 us
    pallas_call x1, Pallas kernels: 82.3 us -> 79.6 us  [per_device(): pl.pallas_call(kernel, out_shape=(jax.ShapeDtypeStruct(field, f32), jax.S...]
where the time goes in v2:
time: 82.3 us; the launch traced here: 82.2 us
  Pallas kernels  79.6 us (97%)
  local copies, waits for them, and re-layouts  1.96 us (2%)
    pallas_call x1, Pallas kernels, per_device(): pl.pallas_call(kernel, out_shape=(jax.ShapeDtypeStruct(field, f32), jax.S...  79.6 us
    unnamed x4, local copies, waits for them, and re-layouts  1.96 us

profile of v2, /device:TPU:1, one launch (start us, length us, event | category | flops | bytes accessed | tf_op | source)
XLA Modules:
  0.0 82.2 jit_solution(8195163989737159267)
XLA Ops:
  0.6 79.6 %shard_map.50 = (f32[6,8,128]{2,1,0:T(8,128)}, f32[6,8,128]{2,1,0:T(8,128)}) custom-call(f32[6,8,128]{2,1,0:T(8,128)} %bitcast.7, bf16[2,4,18,8,128]{4,3,2,1,0:T(8,128)(2,1)} %bitcast.5, bf16[2,4,18,8,128]{4,3,2,1,0:T(8,128)(2,1)} %bitcast.6), custom_call_target="tpu_custom_call" | custom-call | tf_op jit(solution)/shard_map/pallas_call | solution.py:414
  80.2 0.0 copy-start
  80.2 1.4 %copy.7 = f32[2,3,2,4,128]{4,3,2,1,0:T(4,128)} copy(f32[2,3,2,4,128]{4,3,2,1,0:T(4,128)} %bitcast.9) | data formatting | bytes 49152
  81.6 0.0 copy-done
  81.6 0.6 copy.8
Async XLA Ops:
  80.2 1.4 %copy-start = (f32[6,8,128]{2,1,0:T(8,128)S(1)}, f32[6,8,128]{2,1,0:T(8,128)}, u32[]{:S(2)}) copy-start(f32[6,8,128]{2,1,0:T(8,128)} %get-tuple-element.5) | copy-start | bytes 73732

commit v3 on v2

--- a/solution.py
+++ b/solution.py
@@ -84,6 +84,7 @@
     images,
     odd_f,
     mats,
+    products,
     halo,
     rims,
     row,
@@ -126,7 +127,10 @@
             pl.semaphore_signal(barrier, inc=1, device_id=at(axis, by), device_id_type=mesh_id)
     loads = [
         pltpu.make_async_copy(a, c, load.at[n])
-        for n, (a, c) in enumerate(((b_hbm, src_b), (fat_hbm, fat_ref), (long_hbm, long_ref)))
+        for n, (a, c) in enumerate(
+            [(b_hbm, src_b)]
+            + [(a.at[p], c.at[p]) for p in (0, 1) for a, c in ((fat_hbm, fat_ref), (long_hbm, long_ref))]
+        )
     ]
     for c in loads:
         c.start()
@@ -219,6 +223,15 @@
             im = im + mr * vi[j][None] + mi * vr[j][None]
         return re, im
 
+    def local_products(src, dst, select):
+        acc = (jnp.zeros((3, *TILE), jnp.float32),) * 2
+        for n, (_, by) in enumerate(X_HOPS):
+            acc = times(acc, dst, n, along_x(g, by, src))
+        for mu, axis in enumerate(AXES):
+            for kind in range(2):
+                acc = times(acc, dst, 4 + 4 * mu + kind, turn(g, axis, kind, src, select))
+        return acc
+
     def half(fields, dst, hook=None, border_hook=None):
         slot = dst
         copies = halo_copies(fields, slot)
@@ -227,16 +240,7 @@
         if hook is not None:
             hook()
         select = selected(dst)
-        accs = []
-        for field in fields:
-            src = field[...]
-            acc = (jnp.zeros((3, *TILE), jnp.float32),) * 2
-            for n, (_, by) in enumerate(X_HOPS):
-                acc = times(acc, dst, n, along_x(g, by, src))
-            for mu, axis in enumerate(AXES):
-                for kind in range(2):
-                    acc = times(acc, dst, 4 + 4 * mu + kind, turn(g, axis, kind, src, select))
-            accs.append(acc)
+        accs = [local_products(field[...], dst, select) for field in fields]
         if border_hook is not None:
             border_hook()
         per_axis = 2 * len(fields)
@@ -360,23 +364,77 @@
     kept[...] = jnp.zeros_like(kept)
     shift[...] = jnp.zeros_like(shift)
 
-    def first_links():
+    def to_neighbour(src, field, n, side):
+        return pltpu.make_async_remote_copy(
+            src_ref=src,
+            dst_ref=halo.at[1, field, n, side],
+            send_sem=halo_send.at[1, field, n, side],
+            recv_sem=halo_recv.at[1, field, n, side],
+            device_id=at(AXES[n], 2 * side - 1),
+            device_id_type=mesh_id,
+        )
+
+    def adjoint_product(links, mu, src):
+        re = im = jnp.zeros((3, *TILE), jnp.float32)
+        for i in range(3):
+            lr = links[0, mu, pl.ds(3 * i, 3)].astype(jnp.float32)
+            li = links[0, mu, pl.ds(9 + 3 * i, 3)].astype(jnp.float32)
+            vr, vi = src[i][None], src[3 + i][None]
+            re = re - lr * vr - li * vi
+            im = im - lr * vi + li * vr
+        return jnp.concatenate([re, im], axis=0)
+
+    def opening_half():
+        select = selected(1)
+        forth = [to_neighbour(src_b, 0, n, 0) for n in range(3)]
+        for c in forth:
+            c.start()
         loads[1].wait()
         loads[2].wait()
-        for copies in rim:
-            for c in copies:
+        src = src_b[...]
+        back = []
+        for n in range(3):
+            for kind in range(2):
+                products[n, kind] = adjoint_product(kinds[1 - kind], n, src)
+                back.append(to_neighbour(products.at[n, kind], kind, n, 1))
+        for c in back:
+            c.start()
+        loads[3].wait()
+        loads[4].wait()
+        for p in (1, 0):
+            for c in rim[p]:
                 c.start()
         local_matrices(1)
-
-    def second_borders():
-        border_matrices(0)
+        for mu, axis in enumerate(AXES):
+            for kind in range(2):
+                links = plain(kinds[kind], 1, mu)
+                mats[1, 6 + 4 * mu + kind] = jnp.where(
+                    inside(g, axis, kind, select), jnp.zeros_like(links), links
+                )
+        acc = local_products(src, 1, select)
+        for axis, mu in (("gz", 1), ("gy", 2), ("ta", 0)):
+            forth[mu].wait_recv()
+            ahead = halo[1, 0, mu, 0]
+            for kind in range(2):
+                v = across(g, axis, kind, ahead, ahead, select)
+                re, im = times(acc, 1, 6 + 4 * mu + kind, v)
+                back[2 * mu + kind].wait_recv()
+                made = turn(g, axis, kind, halo[1, kind, mu, 1], select)
+                made = jnp.where(inside(g, axis, kind, select), made, 0.0)
+                acc = (re + made[:3], im + made[3:])
+        odd_f[0] = jnp.concatenate(acc, axis=0)
+        for c in forth + back:
+            c.wait_send()
+
+    def link_sends_end():
         for copies in rim:
             for c in copies:
                 c.wait_send()
 
-    first_half([src_b], first_links, lambda: border_matrices(1))
-    (vec[1],) = second_half([src_b], MASS, lambda: local_matrices(0), second_borders)
-    first_half([vec.at[1]])
+    opening_half()
+    (vec[1],) = second_half([src_b], MASS, lambda: local_matrices(0), lambda: border_matrices(0))
+    link_sends_end()
+    first_half([vec.at[1]], None, lambda: border_matrices(1))
     (vec[2],) = second_half([vec.at[1]], MASS)
 
     def block(blk, carry):
@@ -413,7 +471,7 @@
     hbm = pl.BlockSpec(memory_space=pltpu.HBM)
     x, t = pl.pallas_call(
         kernel,
-        out_shape=(jax.ShapeDtypeStruct(field, f32), jax.ShapeDtypeStruct(field, f32)),
+        out_shape=(pltpu.VMEM(field, f32), pltpu.VMEM(field, f32)),
         in_specs=[hbm] * 3,
         out_specs=(vmem, vmem),
         scratch_shapes=[
@@ -426,13 +484,14 @@
             pltpu.VMEM((2, *field), f32),
             pltpu.VMEM((2, *field), f32),
             pltpu.VMEM((2, 16, 18, *TILE), f32),
+            pltpu.VMEM((3, 2, *field), f32),
             pltpu.VMEM((2, 2, 3, 2, *field), f32),
             pltpu.VMEM((2, 3, 2, 18, *TILE), jnp.bfloat16),
             pltpu.VMEM((1, 128), f32),
             pltpu.VMEM((2, BLOCKS, MEMBERS, 1, 128), f32),
             pltpu.VMEM(TILE, f32),
             pltpu.VMEM(TILE, f32),
-            dma((3,)),
+            dma((5,)),
             dma((2, 2, 3, 2)),
             dma((2, 2, 3, 2)),
             dma((2, 3, 2)),

time: 82.3 us -> 80.1 us (0.973)
  Pallas kernels: 79.6 us -> 78.2 us
    pallas_call x1, Pallas kernels: 79.6 us -> 78.2 us  [per_device(): pl.pallas_call(kernel, out_shape=(pltpu.VMEM(field, f32), pltpu.VMEM(fiel...]
    unnamed x4 -> x2, local copies, waits for them, and re-layouts: 1.96 us -> 1.22 us
where the time goes in v3:
time: 80.1 us; the launch traced here: 80 us
  Pallas kernels  78.2 us (98%)
  local copies, waits for them, and re-layouts  1.22 us (2%)
    pallas_call x1, Pallas kernels, per_device(): pl.pallas_call(kernel, out_shape=(pltpu.VMEM(field, f32), pltpu.VMEM(fiel...  78.2 us

profile of v3, /device:TPU:1, one launch (start us, length us, event | category | flops | bytes accessed | tf_op | source)
XLA Modules:
  0.0 80.0 jit_solution(334184914568015677)
XLA Ops:
  0.6 78.2 %shard_map.50 = (f32[6,8,128]{2,1,0:T(8,128)S(1)}, f32[6,8,128]{2,1,0:T(8,128)S(1)}) custom-call(f32[6,8,128]{2,1,0:T(8,128)} %bitcast.9, bf16[2,4,18,8,128]{4,3,2,1,0:T(8,128)(2,1)} %bitcast.7, bf16[2,4,18,8,128]{4,3,2,1,0:T(8,128)(2,1)} %bitcast.8), custom_call_target="tpu_custom_call" | custom-call | tf_op jit(solution)/shard_map/pallas_call | solution.py:472
  78.8 0.6 copy.7
  79.4 0.6 copy.8

commit v4 on v3

--- a/solution.py
+++ b/solution.py
@@ -136,11 +136,11 @@
         c.start()
     pl.semaphore_wait(barrier, 2 * len(AXES))
 
-    def halo_copies(fields, slot):
+    def halo_copies(fields, slot, base=0):
         copies = []
         for n, axis in enumerate(AXES):
             for side, by in enumerate((-1, 1)):
-                for f, src in enumerate(fields):
+                for f, src in enumerate(fields, base):
                     copies.append(
                         pltpu.make_async_remote_copy(
                             src_ref=src,
@@ -232,9 +232,20 @@
                 acc = times(acc, dst, 4 + 4 * mu + kind, turn(g, axis, kind, src, select))
         return acc
 
-    def half(fields, dst, hook=None, border_hook=None):
-        slot = dst
-        copies = halo_copies(fields, slot)
+    def border_products(accs, copies, dst, select, base=0):
+        per_axis = 2 * len(accs)
+        for axis, mu in (("gz", 1), ("gy", 2), ("ta", 0)):
+            for c in copies[per_axis * mu : per_axis * (mu + 1)]:
+                c.wait_recv()
+            for f in range(len(accs)):
+                ahead, behind = halo[dst, base + f, mu, 0], halo[dst, base + f, mu, 1]
+                for kind in range(2):
+                    v = across(g, axis, kind, ahead, behind, select)
+                    accs[f] = times(accs[f], dst, 6 + 4 * mu + kind, v)
+        return [jnp.concatenate(acc, axis=0) for acc in accs]
+
+    def half(fields, dst, hook=None, border_hook=None, base=0):
+        copies = halo_copies(fields, dst, base)
         for c in copies:
             c.start()
         if hook is not None:
@@ -243,18 +254,23 @@
         accs = [local_products(field[...], dst, select) for field in fields]
         if border_hook is not None:
             border_hook()
-        per_axis = 2 * len(fields)
-        for axis, mu in (("gz", 1), ("gy", 2), ("ta", 0)):
-            for c in copies[per_axis * mu : per_axis * (mu + 1)]:
-                c.wait_recv()
-            for f in range(len(fields)):
-                ahead, behind = halo[slot, f, mu, 0], halo[slot, f, mu, 1]
-                for kind in range(2):
-                    v = across(g, axis, kind, ahead, behind, select)
-                    accs[f] = times(accs[f], dst, 6 + 4 * mu + kind, v)
+        out = border_products(accs, copies, dst, select, base)
         for c in copies:
             c.wait_send()
-        return [jnp.concatenate(acc, axis=0) for acc in accs]
+        return out
+
+    def two_halves(fields, others, hook):
+        copies, more = halo_copies(fields, 0), halo_copies(others, 1, 1)
+        for c in copies + more:
+            c.start()
+        hook()
+        accs = [local_products(field[...], 0, selected(0)) for field in fields]
+        rest = [local_products(field[...], 1, selected(1)) for field in others]
+        out = border_products(accs, copies, 0, selected(0))
+        rest = border_products(rest, more, 1, selected(1), 1)
+        for c in copies + more:
+            c.wait_send()
+        return out, rest
 
     def first_half(fields, hook=None, border_hook=None):
         for f, value in enumerate(half(fields, 1, hook, border_hook)):
@@ -295,19 +311,66 @@
 
     lane = lax.broadcasted_iota(jnp.int32, (1, 128), 1)
 
+    def line_of(pairs):
+        rows = [jnp.sum(a * b, axis=0) for a, b in pairs]
+        totals = jnp.sum(jnp.stack(rows), axis=1)
+        totals = jnp.sum(totals, axis=1, keepdims=True)
+        wide = (len(pairs), 128)
+        own_lane = lax.broadcasted_iota(jnp.int32, wide, 0) == lax.broadcasted_iota(jnp.int32, wide, 1)
+        return jnp.sum(jnp.where(own_lane, totals, 0.0), axis=0, keepdims=True)
+
     def local_dots():
         r, w, q = vec[0], vec[1], vec[2]
         m, v = prev[0], prev[1]
-        pairs = ((r, r), (r, w), (w, w), (w, q), (r, m), (w, m), (w, v), (m, m), (m, v))
-        line = jnp.zeros((1, 128), jnp.float32)
-        for n, (a, b) in enumerate(pairs):
-            line = line + jnp.where(lane == n, jnp.sum(jnp.sum(a * b, axis=0)), 0.0)
-        return line
-
-    def coefficients(line):
-        rr, rw, ww, wq, rm, wm, wv, mm, mv = (
-            jnp.broadcast_to(jnp.sum(jnp.where(lane == n, line, 0.0)), TILE) for n in range(DOTS)
-        )
+        return line_of(((r, r), (r, w), (w, w), (w, q), (r, m), (w, m), (w, v), (m, m), (m, v)))
+
+    def moments():
+        pairs = [(vec[(k + 1) // 2], vec[k // 2]) for k in range(7)]
+        odd = odd_f[0]
+        pairs += [(odd, odd)]
+        pairs += [(vec[(k + 1) // 2], prev[k // 2]) for k in range(7)]
+        pairs += [(prev[(k + 1) // 2], prev[k // 2]) for k in range(6)]
+        return line_of(pairs)
+
+    def spread(line, n):
+        return jnp.broadcast_to(jnp.sum(jnp.where(lane == n, line, 0.0)), TILE)
+
+    def times_each(a, b):
+        out = [None] * (len(a) + len(b) - 1)
+        for i, x in enumerate(a):
+            for j, y in enumerate(b):
+                out[i + j] = x * y if out[i + j] is None else out[i + j] + x * y
+        return out
+
+    def plus_each(a, b):
+        return [x + y for x, y in zip(a, b)]
+
+    def dots_from(line, both_steps, c):
+        (_, _, u, f, h), (_, _, u1, f1, h1) = both_steps
+        all_of = [spread(line, n) for n in range(21)]
+        mu, nu, ka = all_of[:8], all_of[8:15], all_of[15:]
+        mu[7] = mu[7] + (MASS - c) * mu[6]
+        p5, q5 = [u, f], [h]
+        p6, q6 = [u1 * u + h1, u1 * f + f1 * u, f1 * f], [u1 * h, f1 * h]
+
+        def forms(p, q, p_, q_, powers):
+            pp, qq = times_each(p, p_), times_each(q, q_)
+            pq = plus_each(times_each(p, q_) + [jnp.zeros_like(u)] * 4, times_each(q, p_) + [jnp.zeros_like(u)] * 4)
+            pq = pq[: max(len(p) + len(q_), len(q) + len(p_)) - 1]
+            for k in powers:
+                terms = [(a, m[n + k]) for s, m in ((pp, mu), (pq, nu), (qq, ka)) for n, a in enumerate(s)]
+                total = terms[0][0] * terms[0][1]
+                for a, m in terms[1:]:
+                    total = total + a * m
+                yield total
+
+        rr, rw, ww, wq = forms(p6, q6, p6, q6, range(4))
+        rm, wm, wv = forms(p6, q6, p5, q5, range(3))
+        mm, mv = forms(p5, q5, p5, q5, range(2))
+        return rr, rw, ww, wq, rm, wm, wv, mm, mv
+
+    def coefficients(dots):
+        rr, rw, ww, wq, rm, wm, wv, mm, mv = dots
         c = shift[...]
         step = rr / (rw + c * rr)
         scale = 1.0 / (1.0 - step * rr * kept[...])
@@ -322,13 +385,12 @@
         return (step, scale, u, f, h), (step1, scale1, u1, f1, h1), mean1
 
     def early_update(line):
-        (step, scale, u, f, h), (step1, scale1, u1, f1, h1), mean1 = coefficients(line)
+        (step, scale, u, f, h), (step1, scale1, u1, f1, h1), mean1 = coefficients(
+            [spread(line, n) for n in range(DOTS)]
+        )
         first = [u * vec[k] + f * vec[k + 1] + h * prev[k] for k in range(3)]
         second = [u1 * first[k] + f1 * first[k + 1] + h1 * vec[k] for k in range(2)]
-        x, x0 = xs[0], xs[1]
-        x1 = scale * (x + step * vec[0]) + h * x0
-        xs[1] = x1
-        xs[0] = scale1 * (x1 + step1 * first[0]) + h1 * x
+        iterates(((step, scale, u, f, h), (step1, scale1, u1, f1, h1)), first[0])
         d = mean1 - shift[...]
         shift[...] = mean1
         half_first3 = u * vec[3] + h * prev[3]
@@ -344,10 +406,16 @@
                 place[k] = stack[0]
                 stack = [b - d * a for a, b in zip(stack, stack[1:])]
 
-    def last_update(line):
-        (step, scale, u, f, h), (step1, scale1, u1, f1, h1), _ = coefficients(line)
+    def iterates(both_steps, first):
+        (step, scale, _, _, h), (step1, scale1, _, _, h1) = both_steps
+        x, x0 = xs[0], xs[1]
+        x1 = scale * (x + step * vec[0]) + h * x0
+        xs[1] = x1
+        xs[0] = scale1 * (x1 + step1 * first) + h1 * x
+
+    def last_update(dots, r, w, q, m, v):
+        (step, scale, u, f, h), (step1, scale1, u1, f1, h1), _ = coefficients(dots)
         c = shift[...]
-        r, w, q, m, v = vec[0], vec[1], vec[2], prev[0], prev[1]
         x, x0, ax, ax0 = xs[0], xs[1], images[0], images[1]
         r1 = u * r + f * w + h * m
         x1 = scale * (x + step * r) + h * x0
@@ -451,14 +519,43 @@
         late_update(parts, fourth)
         return carry
 
-    lax.fori_loop(0, BLOCKS - 1, block, 0)
-    last = BLOCKS - 1
+    lax.fori_loop(0, BLOCKS - 2, block, 0)
+
+    blk, last = BLOCKS - 2, BLOCKS - 1
+    c = shift[...]
+    first_half([vec.at[2]], lambda: stage_start(blk, 0, local_dots()))
+    (vec[3],) = second_half(
+        [vec.at[2]], MASS - c, lambda: stage_start(blk, 1, stage_end(blk, 0))
+    )
+    known = []
+
+    def steps_and_iterates():
+        line = stage_end(blk, 1)
+        a, b, _ = coefficients([spread(line, n) for n in range(DOTS)])
+        known.extend((a, b))
+        iterates(known, a[2] * vec[0] + a[3] * vec[1] + a[4] * prev[0])
+
+    first_half([vec.at[3]], steps_and_iterates)
     both = [xs.at[0], xs.at[1]]
-    first_half(both, lambda: stage_start(last, 0, local_dots()))
-    images[0], images[1] = second_half(
-        both, MASS, lambda: stage_start(last, 1, stage_end(last, 0))
+    (value,), odds = two_halves(
+        [odd_f.at[0]], both, lambda: stage_start(last, 0, moments())
     )
-    last_update(stage_end(last, 1))
+    odd_f[1], odd_f[2] = odds
+    fourth = (MASS - c) * vec[3] - value
+    (_, _, u, f, h), (_, _, u1, f1, h1) = known
+    powers = [vec[0], vec[1], vec[2], vec[3], fourth]
+    before = [u * powers[k] + f * powers[k + 1] + h * prev[k] for k in range(4)]
+    after = [u1 * before[k] + f1 * before[k + 1] + h1 * powers[k] for k in range(3)]
+    values = half(
+        [odd_f.at[1], odd_f.at[2]],
+        0,
+        lambda: stage_start(last, 1, stage_end(last, 0)),
+        None,
+        1,
+    )
+    for n in range(2):
+        images[n] = MASS * xs[n] - values[n]
+    last_update(dots_from(stage_end(last, 1), known, c), *after, *before[:2])
 
 
 def per_device(source, fat_links, long_links):
@@ -482,18 +579,18 @@
             pltpu.VMEM((4, *field), f32),
             pltpu.VMEM((2, *field), f32),
             pltpu.VMEM((2, *field), f32),
-            pltpu.VMEM((2, *field), f32),
+            pltpu.VMEM((3, *field), f32),
             pltpu.VMEM((2, 16, 18, *TILE), f32),
             pltpu.VMEM((3, 2, *field), f32),
-            pltpu.VMEM((2, 2, 3, 2, *field), f32),
+            pltpu.VMEM((2, 3, 3, 2, *field), f32),
             pltpu.VMEM((2, 3, 2, 18, *TILE), jnp.bfloat16),
             pltpu.VMEM((1, 128), f32),
             pltpu.VMEM((2, BLOCKS, MEMBERS, 1, 128), f32),
             pltpu.VMEM(TILE, f32),
             pltpu.VMEM(TILE, f32),
             dma((5,)),
-            dma((2, 2, 3, 2)),
-            dma((2, 2, 3, 2)),
+            dma((2, 3, 3, 2)),
+            dma((2, 3, 3, 2)),
             dma((2, 3, 2)),
             dma((2, 3, 2)),
             dma((MEMBERS - 1,)),

time: 80.1 us -> 77.2 us (0.964)
  Pallas kernels: 78.2 us -> 75.3 us
    pallas_call x1, Pallas kernels: 78.2 us -> 75.3 us  [per_device(): pl.pallas_call(kernel, out_shape=(pltpu.VMEM(field, f32), pltpu.VMEM(fiel...]
where the time goes in v4:
time: 77.2 us; the launch traced here: 77.1 us
  Pallas kernels  75.3 us (98%)
  local copies, waits for them, and re-layouts  1.22 us (2%)
    pallas_call x1, Pallas kernels, per_device(): pl.pallas_call(kernel, out_shape=(pltpu.VMEM(field, f32), pltpu.VMEM(fiel...  75.3 us

profile of v4, /device:TPU:1, one launch (start us, length us, event | category | flops | bytes accessed | tf_op | source)
XLA Modules:
  0.0 77.1 jit_solution(3388886053738697431)
XLA Ops:
  0.6 75.3 %shard_map.50 = (f32[6,8,128]{2,1,0:T(8,128)S(1)}, f32[6,8,128]{2,1,0:T(8,128)S(1)}) custom-call(f32[6,8,128]{2,1,0:T(8,128)} %bitcast.9, bf16[2,4,18,8,128]{4,3,2,1,0:T(8,128)(2,1)} %bitcast.7, bf16[2,4,18,8,128]{4,3,2,1,0:T(8,128)(2,1)} %bitcast.8), custom_call_target="tpu_custom_call" | custom-call | tf_op jit(solution)/shard_map/pallas_call | solution.py:569
  75.9 0.6 copy.7
  76.5 0.6 copy.8

commit v5 on v4

--- a/solution.py
+++ b/solution.py
@@ -261,9 +261,9 @@
 
     def two_halves(fields, others, hook):
         copies, more = halo_copies(fields, 0), halo_copies(others, 1, 1)
+        hook()
         for c in copies + more:
             c.start()
-        hook()
         accs = [local_products(field[...], 0, selected(0)) for field in fields]
         rest = [local_products(field[...], 1, selected(1)) for field in others]
         out = border_products(accs, copies, 0, selected(0))
@@ -326,8 +326,6 @@
 
     def moments():
         pairs = [(vec[(k + 1) // 2], vec[k // 2]) for k in range(7)]
-        odd = odd_f[0]
-        pairs += [(odd, odd)]
         pairs += [(vec[(k + 1) // 2], prev[k // 2]) for k in range(7)]
         pairs += [(prev[(k + 1) // 2], prev[k // 2]) for k in range(6)]
         return line_of(pairs)
@@ -348,7 +346,7 @@
     def dots_from(line, both_steps, c):
         (_, _, u, f, h), (_, _, u1, f1, h1) = both_steps
         all_of = [spread(line, n) for n in range(21)]
-        mu, nu, ka = all_of[:8], all_of[8:15], all_of[15:]
+        mu, nu, ka = all_of[:7] + all_of[20:], all_of[7:14], all_of[14:20]
         mu[7] = mu[7] + (MASS - c) * mu[6]
         p5, q5 = [u, f], [h]
         p6, q6 = [u1 * u + h1, u1 * f + f1 * u, f1 * f], [u1 * h, f1 * h]
@@ -532,27 +530,26 @@
     def steps_and_iterates():
         line = stage_end(blk, 1)
         a, b, _ = coefficients([spread(line, n) for n in range(DOTS)])
-        known.extend((a, b))
-        iterates(known, a[2] * vec[0] + a[3] * vec[1] + a[4] * prev[0])
+        iterates((a, b), a[2] * vec[0] + a[3] * vec[1] + a[4] * prev[0])
+        known.extend((a, b, moments()))
 
     first_half([vec.at[3]], steps_and_iterates)
+    ready = known.pop()
     both = [xs.at[0], xs.at[1]]
-    (value,), odds = two_halves(
-        [odd_f.at[0]], both, lambda: stage_start(last, 0, moments())
-    )
+
+    def last_moment():
+        odd = odd_f[0]
+        stage_start(last, 0, ready + jnp.where(lane == 20, jnp.sum(odd * odd), 0.0))
+
+    (value,), odds = two_halves([odd_f.at[0]], both, last_moment)
     odd_f[1], odd_f[2] = odds
     fourth = (MASS - c) * vec[3] - value
     (_, _, u, f, h), (_, _, u1, f1, h1) = known
     powers = [vec[0], vec[1], vec[2], vec[3], fourth]
     before = [u * powers[k] + f * powers[k + 1] + h * prev[k] for k in range(4)]
     after = [u1 * before[k] + f1 * before[k + 1] + h1 * powers[k] for k in range(3)]
-    values = half(
-        [odd_f.at[1], odd_f.at[2]],
-        0,
-        lambda: stage_start(last, 1, stage_end(last, 0)),
-        None,
-        1,
-    )
+    stage_start(last, 1, stage_end(last, 0))
+    values = half([odd_f.at[1], odd_f.at[2]], 0, base=1)
     for n in range(2):
         images[n] = MASS * xs[n] - values[n]
     last_update(dots_from(stage_end(last, 1), known, c), *after, *before[:2])

time: 77.2 us -> 77.1 us (level)
  no operation moved by 1% of the time
where the time goes in v5:
time: 77.1 us; the launch traced here: 77 us
  Pallas kernels  75.2 us (98%)
  local copies, waits for them, and re-layouts  1.22 us (2%)
    pallas_call x1, Pallas kernels, per_device(): pl.pallas_call(kernel, out_shape=(pltpu.VMEM(field, f32), pltpu.VMEM(fiel...  75.2 us

profile of v5, /device:TPU:1, one launch (start us, length us, event | category | flops | bytes accessed | tf_op | source)
XLA Modules:
  0.0 77.0 jit_solution(1682486664302587513)
XLA Ops:
  0.6 75.2 %shard_map.50 = (f32[6,8,128]{2,1,0:T(8,128)S(1)}, f32[6,8,128]{2,1,0:T(8,128)S(1)}) custom-call(f32[6,8,128]{2,1,0:T(8,128)} %bitcast.9, bf16[2,4,18,8,128]{4,3,2,1,0:T(8,128)(2,1)} %bitcast.7, bf16[2,4,18,8,128]{4,3,2,1,0:T(8,128)(2,1)} %bitcast.8), custom_call_target="tpu_custom_call" | custom-call | tf_op jit(solution)/shard_map/pallas_call | solution.py:566
  75.8 0.6 copy.7
  76.4 0.6 copy.8

commit v6 on v5

--- a/solution.py
+++ b/solution.py
@@ -331,7 +331,7 @@
         return line_of(pairs)
 
     def spread(line, n):
-        return jnp.broadcast_to(jnp.sum(jnp.where(lane == n, line, 0.0)), TILE)
+        return jnp.broadcast_to(line[:, n : n + 1], TILE)
 
     def times_each(a, b):
         out = [None] * (len(a) + len(b) - 1)

time: 77.1 us -> 77.1 us (level)
  no operation moved by 1% of the time
where the time goes in v6:
time: 77.1 us; the launch traced here: 77 us
  Pallas kernels  75.2 us (98%)
  local copies, waits for them, and re-layouts  1.22 us (2%)
    pallas_call x1, Pallas kernels, per_device(): pl.pallas_call(kernel, out_shape=(pltpu.VMEM(field, f32), pltpu.VMEM(fiel...  75.2 us

profile of v6, /device:TPU:1, one launch (start us, length us, event | category | flops | bytes accessed | tf_op | source)
XLA Modules:
  0.0 77.0 jit_solution(2574571599474998847)
XLA Ops:
  0.6 75.2 %shard_map.50 = (f32[6,8,128]{2,1,0:T(8,128)S(1)}, f32[6,8,128]{2,1,0:T(8,128)S(1)}) custom-call(f32[6,8,128]{2,1,0:T(8,128)} %bitcast.9, bf16[2,4,18,8,128]{4,3,2,1,0:T(8,128)(2,1)} %bitcast.7, bf16[2,4,18,8,128]{4,3,2,1,0:T(8,128)(2,1)} %bitcast.8), custom_call_target="tpu_custom_call" | custom-call | tf_op jit(solution)/shard_map/pallas_call | solution.py:566
  75.8 0.6 copy.7
  76.4 0.6 copy.8
